TPU v7x, 128 devices: a whole 4x4x4 slice. The times are simulated.
128 devices in a mesh: row: 8 (over x, core), col: 16 (over z, y).
Axes of the slice: x: 4, y: 4, z: 4, core: 2. Of those that a mesh axis runs over, the one named last changes fastest.
Arguments:
- ham: bfloat16 [6144, 6144], P('row', 'col'), may hold values from -0.078125 to 0.078125
- deriv: bfloat16 [6144, 6144], P('row', 'col'), may hold values from -6 to 6
- band: int32 [48], replicated, may hold values from 1 to 24, as said below
- frag_of: int32 [48], replicated, may hold values from 0 to 31
Outputs:
- sign_iterate: bfloat16 [6144, 6144], P('row', 'col')
- energy_density: bfloat16 [6144, 6144], P('row', 'col')
- pulay_terms: float32 [32, 128], P('col')
Inputs may be any that keep to these rules, and one draw needn't show every extreme that they name: Some block row has band half-width exactly 24.
All inputs are finite; a program needn't handle non-finite values.
Results may differ from a plain program's by a relative error of at most 0.006.
Values may be sent and summed in bfloat16 or wider, within the bound.
A program may use at most 64 MiB of HBM per device.

v0:
```python
import jax
import jax.numpy as jnp
from jax import lax
from jax.sharding import PartitionSpec as P

BLK = 128
FRAG_DEV = 2


def column_panel_of(right_matrix):
    return lax.all_gather(right_matrix, "row", axis=0, tiled=True)


def folded_product(left_matrix, right_matrix):
    whole_panel = column_panel_of(right_matrix)
    return jnp.dot(
        lax.all_gather(left_matrix, "col", axis=1, tiled=True),
        whole_panel,
        preferred_element_type=jnp.float32,
    )


def body(ham, deriv, band, frag_of):
    rows_here = ham.shape[0]
    cols_here = ham.shape[1]
    block_rows = rows_here // BLK
    block_cols = cols_here // BLK
    row_index = lax.axis_index("row")
    col_index = lax.axis_index("col")
    row_blocks = row_index * block_rows + jnp.arange(block_rows, dtype=jnp.int32)
    col_blocks = col_index * block_cols + jnp.arange(block_cols, dtype=jnp.int32)
    row_band = lax.dynamic_slice_in_dim(band, row_index * block_rows, block_rows)
    col_band = lax.dynamic_slice_in_dim(band, col_index * block_cols, block_cols)
    widest = jnp.maximum(row_band[:, None], col_band[None, :])
    inside = jnp.abs(row_blocks[:, None] - col_blocks[None, :]) <= widest
    pattern = jnp.repeat(jnp.repeat(inside.astype(jnp.float32), BLK, axis=0), BLK, axis=1)
    global_rows = row_index * rows_here + jnp.arange(rows_here, dtype=jnp.int32)
    global_cols = col_index * cols_here + jnp.arange(cols_here, dtype=jnp.int32)
    identity = (global_rows[:, None] == global_cols[None, :]).astype(jnp.float32)
    start = (ham.astype(jnp.float32) * pattern).astype(jnp.bfloat16)

    def start_times(right_matrix):
        return folded_product(start, right_matrix)

    square = (start_times(start) * pattern).astype(jnp.bfloat16)
    cubic = start_times(square)
    sign_iterate = (pattern * (1.5 * start.astype(jnp.float32) - 0.5 * cubic)).astype(jnp.bfloat16)
    density = (0.5 * (identity - sign_iterate.astype(jnp.float32))).astype(jnp.bfloat16)
    weighted = (start_times(density) * pattern).astype(jnp.bfloat16)
    energy_density = (folded_product(density, weighted) * pattern).astype(jnp.bfloat16)
    column_terms = jnp.sum(energy_density.astype(jnp.float32) * deriv.astype(jnp.float32), axis=0)
    column_terms = column_terms.reshape(block_cols, BLK)
    local_frags = lax.dynamic_slice_in_dim(frag_of, col_index * block_cols, block_cols)
    fragment_count = FRAG_DEV * lax.axis_size("col")
    fragments = jnp.arange(fragment_count, dtype=jnp.int32)
    onehot = (local_frags[None, :] == fragments[:, None]).astype(jnp.float32)
    partial_value = jnp.dot(onehot, column_terms, precision=lax.Precision.HIGHEST)
    grand_total = lax.psum(partial_value, ("row", "col"))
    pulay_terms = lax.dynamic_slice_in_dim(grand_total, col_index * FRAG_DEV, FRAG_DEV, 0)
    return (sign_iterate, energy_density, pulay_terms)


def solution(mesh):
    placed = (P("row", "col"), P("row", "col"), P(), P())
    return jax.shard_map(
        body,
        mesh=mesh,
        in_specs=placed,
        out_specs=(P("row", "col"), P("row", "col"), P("col", None)),
        check_vma=False,
    )
```

profile of v0, /device:TPU:1, one launch (start us, length us, event | category | flops | bytes accessed | tf_op | source)
XLA Modules:
  0.0 432.5 jit_solution(7368020755092818838)
XLA Ops:
  7.2 0.0 all-gather.9.cloned.1.call-start
  7.2 0.7 dynamic_slice.13
  8.0 0.7 dynamic_slice.12
  8.7 0.1 fusion.9
  8.8 0.1 broadcast_bitcast_fusion
  8.9 0.1 broadcast_in_dim.5
  9.0 0.4 copy.8
  9.3 0.7 copy-done
  10.0 0.9 multiply_convert_fusion.1
  11.0 0.0 all-gather.7.cloned.1.call-start
  11.0 0.7 all-gather.7.cloned.1.call-update
  11.7 0.0 all-gather.11.cloned.1.call-start
  11.8 37.2 %all-gather.9.cloned.1.call-done = bf16[6144,384]{1,0:T(8,128)(2,1)} async-done(((bf16[768,384]{1,0:T(8,128)(2,1)}), bf16[6144,384]{1,0:T(8,128)(2,1)}) %all-gather.9.cloned.1.call-update) | async-done | bytes 4718608 | tf_op jit(solution)/shard_map/all_gather | solution.py:11
  48.9 83.6 %all-gather.7.cloned.1.call-done = bf16[768,6144]{1,0:T(8,128)(2,1)} async-done(((bf16[768,384]{1,0:T(8,128)(2,1)}), bf16[768,6144]{1,0:T(8,128)(2,1)}) %all-gather.7.cloned.1.call-update) | async-done | bytes 9437200 | tf_op jit(solution)/shard_map/all_gather | solution.py:17
  132.5 9.7 %fusion.3 = bf16[768,384]{0,1:T(8,128)(2,1)} fusion(f32[768,384]{0,1:T(8,128)S(1)} %bitcast.20, bf16[768,6144]{1,0:T(8,128)(2,1)} %all-gather.7.cloned.1.call-done, bf16[6144,384]{1,0:T(8,128)(2,1)} %all-gather.9.cloned.1.call-done), kind=kOutput, calls=%fused_computation.7 | convolution fusion | flops 3624468480 | bytes 15925248 | tf_op jit(solution)/shard_map/dot_general | solution.py:16
  142.2 0.0 all-gather.11.cloned.1.call-update
  142.3 0.0 all-gather.15.cloned.1.call-start
  142.3 35.3 %all-gather.11.cloned.1.call-done = bf16[6144,384]{0,1:T(8,128)(2,1)} async-done(((bf16[768,384]{0,1:T(8,128)(2,1)}), bf16[6144,384]{0,1:T(8,128)(2,1)}) %all-gather.11.cloned.1.call-update) | async-done | bytes 4718608 | tf_op jit(solution)/shard_map/all_gather | solution.py:11
  177.6 10.0 %multiply_convert_fusion = (bf16[768,384]{1,0:T(8,128)(2,1)}, bf16[768,384]{1,0:T(8,128)(2,1)}) fusion(s32[384]{0:T(512)S(1)} %iota_add_fusion.1, s32[768]{0:T(1024)S(1)} %iota_add_fusion, f32[768,384]{1,0:T(8,128)S(1)} %copy.8, bf16[768,6144]{1,0:T(8,128)(2,1)} %all-gather.7.cloned.1.call-done, bf16[6144,384]{0,1:T(8,128)(2,1)} %all-gather.11.cloned.1.call-done, ...), kind=kOutput, calls=%fused_computation.11 | convolution fusion | flops 3628302336 | bytes 17109504 | tf_op jit(solution)/shard_map/dot_general | solution.py:16
  187.6 0.0 all-gather.17.cloned.1.call-start
  187.7 34.3 %all-gather.15.cloned.1.call-done = bf16[6144,384]{1,0:T(8,128)(2,1)} async-done(((bf16[768,384]{1,0:T(8,128)(2,1)}), bf16[6144,384]{1,0:T(8,128)(2,1)}) %all-gather.15.cloned.1.call-update) | async-done | bytes 4718608 | tf_op jit(solution)/shard_map/all_gather | solution.py:11
  222.0 9.7 %fusion.4 = bf16[768,384]{0,1:T(8,128)(2,1)} fusion(f32[768,384]{0,1:T(8,128)S(1)} %bitcast.21, bf16[768,6144]{1,0:T(8,128)(2,1)} %all-gather.7.cloned.1.call-done, bf16[6144,384]{1,0:T(8,128)(2,1)} %all-gather.15.cloned.1.call-done), kind=kOutput, calls=%fused_computation.8 | convolution fusion | flops 3624468480 | bytes 15925248 | tf_op jit(solution)/shard_map/dot_general | solution.py:16
  231.7 0.2 all-gather.13.cloned.1.call-start
  231.9 0.3 all-gather.13.cloned.1.call-update
  232.3 0.0 copy-done.2
  232.3 0.1 dynamic_slice.14
  232.4 33.7 %all-gather.17.cloned.1.call-done = bf16[6144,384]{0,1:T(8,128)(2,1)} async-done(((bf16[768,384]{0,1:T(8,128)(2,1)}), bf16[6144,384]{0,1:T(8,128)(2,1)}) %all-gather.17.cloned.1.call-update) | async-done | bytes 4718608 | tf_op jit(solution)/shard_map/all_gather | solution.py:11
  266.1 83.4 %all-gather.13.cloned.1.call-done = bf16[768,6144]{1,0:T(8,128)(2,1)} async-done(((bf16[768,384]{1,0:T(8,128)(2,1)}), bf16[768,6144]{1,0:T(8,128)(2,1)}) %all-gather.13.cloned.1.call-update) | async-done | bytes 9437200 | tf_op jit(solution)/shard_map/all_gather | solution.py:17
  349.5 9.8 %multiply_reduce_fusion = (f32[384]{0:T(512)S(1)}, bf16[768,384]{1,0:T(8,128)(2,1)}) fusion(bf16[768,384]{1,0:T(8,128)(2,1)S(1)} %copy-done.1, f32[768,384]{1,0:T(8,128)S(1)} %copy.8, bf16[768,6144]{1,0:T(8,128)(2,1)} %all-gather.13.cloned.1.call-done, bf16[6144,384]{0,1:T(8,128)(2,1)} %all-gather.17.cloned.1.call-done), kind=kOutput, calls=%fused_computation.10 | convolution fusion | flops 3625647616 | bytes 16516608 | tf_op jit(solution)/shard_map/dot_general | solution.py:16
  359.3 0.1 fusion.6
  359.4 65.7 %psum.7 = f32[32,128]{1,0:T(8,128)S(1)} all-reduce(f32[32,128]{1,0:T(8,128)S(1)} %fusion.6), channel_id=1, replica_groups=mesh['row'=8,'col'=16] {'row','col'}, use_global_device_ids=true, to_apply=%region_1.0 | all-reduce | flops 4096 | bytes 32768 | tf_op jit(solution)/shard_map/psum | solution.py:58
  425.1 0.6 constant_dynamic-slice_fusion
  (12 shorter events, 0.1 us)
Async XLA Ops:
  7.2 41.8 %all-gather.9.cloned.1.call-start = ((), (), s32[]{:S(2)}) async-start(), calls=%async_computation.1 | async-start | bytes 5308416 | tf_op jit(solution)/shard_map/all_gather | solution.py:11
  9.0 1.1 copy-start
  11.0 121.6 %all-gather.7.cloned.1.call-start = ((), (), s32[]{:S(2)}) async-start(), calls=%async_computation | async-start | bytes 10027008 | tf_op jit(solution)/shard_map/all_gather | solution.py:17
  11.7 165.9 %all-gather.11.cloned.1.call-start = ((), (), s32[]{:S(2)}) async-start(), calls=%async_computation.2 | async-start | bytes 5308416 | tf_op jit(solution)/shard_map/all_gather | solution.py:11
  142.3 79.7 %all-gather.15.cloned.1.call-start = ((), (), s32[]{:S(2)}) async-start(), calls=%async_computation.4 | async-start | bytes 5308416 | tf_op jit(solution)/shard_map/all_gather | solution.py:11
  187.6 78.5 %all-gather.17.cloned.1.call-start = ((), (), s32[]{:S(2)}) async-start(), calls=%async_computation.5 | async-start | bytes 5308416 | tf_op jit(solution)/shard_map/all_gather | solution.py:11
  231.7 0.7 copy-start.2
  231.7 117.8 %copy-start.1 = (bf16[768,384]{1,0:T(8,128)(2,1)S(1)}, bf16[768,384]{1,0:T(8,128)(2,1)}, u32[]{:S(2)}) copy-start(bf16[768,384]{1,0:T(8,128)(2,1)} %param.5) | copy-start | bytes 1769476
  231.7 117.8 %all-gather.13.cloned.1.call-start = ((), (), s32[]{:S(2)}) async-start(), calls=%async_computation.3 | async-start | bytes 10027008 | tf_op jit(solution)/shard_map/all_gather | solution.py:17
Sparse Core Ops, SparseCore 0:
  11.1 37.7 all-gather.8
  51.6 80.8 all-gather.6
  142.4 35.1 all-gather.10
  187.7 34.2 all-gather.14
  231.8 34.2 all-gather.16
  268.6 80.8 all-gather.12
where the time goes:
time: 433 us
  waiting for transfers between devices  309 us (71%)
  blocking collectives  65.7 us (15%)
  matrix products  39.3 us (9%)
  between operations  14.2 us (3%)
    all_gather x2, waiting for transfers between devices, folded_product(): lax.all_gather(left_matrix, 'col', axis=1, tiled=True)  167 us
    all_gather x4, waiting for transfers between devices, column_panel_of(): return lax.all_gather(right_matrix, 'row', axis=0, tiled=True)  140 us
    psum x1, blocking collectives, body(): grand_total = lax.psum(partial_value, ('row', 'col'))  65.7 us
    dot_general x4, matrix products, folded_product(): jnp.dot(lax.all_gather(left_matrix, 'col', axis=1, tiled=True), whole_pan...  39.1 us
  transfers between devices with their start and end apart: 6, of which 6 were waited for; matrix products, arithmetic and copies ran while one was open for 0% of the time, Pallas kernels for 0%

commit v1 on v0

v1 whole, which is shorter than its diff:
```python
import functools

import jax
import jax.numpy as jnp
from jax import lax
from jax.experimental import pallas as pl
from jax.experimental.pallas import tpu as pltpu
from jax.sharding import PartitionSpec as P

MESH = pl.DeviceIdType.MESH
BLK = 128
ROWS = 768
COLS = 384
NR = 8
NC = 16
F32 = jnp.float32
BF16 = jnp.bfloat16
OFFS = (0, 256, 512, 640)
HALF = (128, 128, 64, 64)
ORDER = (
    "RaS0", "RaS1", "RaS2", "LaS0", "LaS1", "prep", "LbS0", "RbS0", "RaS3", "LbS1", "LcS0", "LaS2",
    "LcS1", "LaS3", "RbS1", "RbS2", "RcS0", "RdS0", "RbS3", "LdS0", "LbS2", "RcS1", "RcS2", "RdS1",
    "RcS3", "RdS2", "RdS3", "LdS1", "LbS3", "LeS0", "P1_0", "LcS2", "RaQ0", "LeS1", "P1_1", "LcS3",
    "RaQ1", "RbQ0", "LdS2", "RbQ1", "LdS3", "RcQ0", "LeS2", "P1_2", "RdQ0", "RaQ2", "RcQ1", "P2_00",
    "LeS3", "P1_3", "RaQ3", "RdQ1", "P2_01", "P2_10", "RbQ2", "P2_11", "P2_20", "P2_21", "RbQ3", "RcQ2",
    "RdQ2", "P2_02", "RcQ3", "P2_12", "P2_22", "RdQ3", "P2_03", "N0", "RaD0", "LaD0", "P2_13", "N1",
    "RaD1", "LaD1", "P2_23", "N2", "RaD2", "N3", "LbD0", "RbD0", "LbD1", "RaD3", "LcD0", "LaD2",
    "LcD1", "LaD3", "RbD1", "RbD2", "RcD0", "RdD0", "P3_00", "LdD0", "RbD3", "P3_10", "LbD2", "P3_20",
    "RcD1", "RcD2", "RcD3", "RdD1", "P3_01", "RdD2", "P3_02", "P3_11", "RdD3", "P3_03", "W0", "RaW0",
    "P3_12", "P3_13", "W1", "RaW1", "P3_21", "P3_22", "P3_23", "W2", "LdD1", "RaW2", "LbD3", "RbW0",
    "RaW3", "LeD0", "LcD2", "RbW1", "RbW2", "LeD1", "LcD3", "RcW0", "RdW0", "P4_00", "RbW3", "P4_10",
    "LdD2", "RcW1", "RcW2", "RdW1", "P4_01", "RdW2", "RcW3", "P4_02", "P4_11", "LdD3", "P4_12", "RdW3",
    "P4_03", "E0", "P4_13", "LeD2", "P4_2", "E2", "E1", "LeD3", "P4_3", "E3",
)


def kernel(band, frag, ham, deriv, n_out, e_out, pulay, ls, ld, rs, rq, rd, rw, mask, acc, terms, mine, by_row, by_col,
           weights, l_send, l_recv, r_send, r_recv, t_send, t_recv):
    r = lax.axis_index("row")
    c = lax.axis_index("col")
    z = lax.div(c, 4)
    y = lax.rem(c, 4)
    up = {"y": lax.rem(y + 1, 4), "z": lax.rem(z + 1, 4)}
    down = {"y": lax.rem(y + 3, 4), "z": lax.rem(z + 3, 4)}
    to = {
        ("y", 0): (r, z * 4 + up["y"]),
        ("y", 1): (r, z * 4 + down["y"]),
        ("z", 0): (r, up["z"] * 4 + y),
        ("z", 1): (r, down["z"] * 4 + y),
        ("x", 0): (lax.rem(r + 2, NR), c),
        ("x", 1): (lax.rem(r + 6, NR), c),
        "core": (r + 1 - 2 * lax.rem(r, 2), c),
    }
    r_up, r_down, r_far = lax.rem(r + 2, NR), lax.rem(r + 6, NR), lax.rem(r + 4, NR)

    barrier = pltpu.get_barrier_semaphore()
    for k in range(1, NR):
        pl.semaphore_signal(barrier, inc=1, device_id=(lax.rem(r + k, NR), c), device_id_type=MESH)
    for k in range(1, NC):
        pl.semaphore_signal(barrier, inc=1, device_id=(r, lax.rem(c + k, NC)), device_id_type=MESH)

    sent = []
    flying = {}

    def send(key, ref, target, send_sem, recv_sem):
        copy = pltpu.make_async_remote_copy(
            src_ref=ref, dst_ref=ref, send_sem=send_sem, recv_sem=recv_sem, device_id=target, device_id_type=MESH
        )
        copy.start()
        sent.append(copy)
        flying[key] = copy

    def landed(key):
        flying[key].wait_recv()

    left = {"S": ls, "D": ld}
    right = {"S": rs, "Q": rq, "D": rd, "W": rw}

    def left_send(x, p, stage, first, side, ref):
        axis = {"A": "yz", "B": "zy"}[first][0 if stage in "ab" else 1]
        i = ((("SD".index(x) * 4 + p) * 4 + "abcd".index(stage)) * 2 + "AB".index(first)) * 2 + side
        send((x, p, stage, first, side), ref, to[axis, side], l_send.at[i], l_recv.at[i])

    def left_wait(x, p, stage):
        for first in "AB":
            for side in (0, 1):
                landed((x, p, stage, first, side))

    def left_step(stage, x, p):
        buf, h, a = left[x], HALF[p], OFFS[p]
        if stage != "a":
            left_wait(x, p, "abcd"["bcde".index(stage)])
        for first in "AB":
            lo = a if first == "A" else a + h
            every = pl.ds(lo, h)
            parts = (pl.ds(lo, h // 2), pl.ds(lo + h // 2, h // 2))
            for side in (0, 1):
                back = (down, up)[side]
                if stage == "a":
                    ref = buf.at[z, y, every]
                elif stage == "b":
                    ref = buf.at[z, back["y"], parts[side]] if first == "A" else buf.at[back["z"], y, parts[side]]
                elif stage == "c":
                    ref = buf.at[z, :, every] if first == "A" else buf.at[:, y, every]
                elif stage == "d":
                    ref = buf.at[back["z"], :, parts[side]] if first == "A" else buf.at[:, back["y"], parts[side]]
                else:
                    return
                left_send(x, p, stage, first, side, ref)

    def right_send(x, p, kind, ref, target):
        i = ("SQDW".index(x) * 4 + p) * 8 + kind
        send((x, p, kind), ref, target, r_send.at[i], r_recv.at[i])

    def right_step(stage, x, p):
        buf, a, n = right[x], OFFS[p], 2 * HALF[p]
        rows = pl.ds(a, n)
        if stage == "a":
            right_send(x, p, 0, buf.at[r, rows], to["x", 0])
            right_send(x, p, 1, buf.at[r, rows], to["x", 1])
            right_send(x, p, 4, buf.at[r, rows], to["core"])
        elif stage == "b":
            landed((x, p, 0))
            landed((x, p, 1))
            right_send(x, p, 2, buf.at[r_down, pl.ds(a, n // 2)], to["x", 0])
            right_send(x, p, 3, buf.at[r_up, pl.ds(a + n // 2, n // 2)], to["x", 1])
            right_send(x, p, 5, buf.at[r_down, rows], to["core"])
            right_send(x, p, 6, buf.at[r_up, rows], to["core"])
        elif stage == "c":
            landed((x, p, 2))
            landed((x, p, 3))
            right_send(x, p, 7, buf.at[r_far, rows], to["core"])
        else:
            for kind in (4, 5, 6, 7):
                landed((x, p, kind))

    def whole(buf, panel, a, n):
        rows = pl.ds(a, n)
        acc[rows, :] = jnp.zeros((n, COLS), F32)

        def step(i, _):
            lhs = jnp.concatenate([buf[i, j, rows, :] for j in range(4)], axis=1)
            rhs = panel[pl.ds(2 * i, 2)].reshape(4 * COLS, COLS)
            acc[rows, :] += jnp.dot(lhs, rhs, preferred_element_type=F32)
            return 0

        lax.fori_loop(0, 4, step, 0)

    def part(buf, panel, a, n, q):
        rows = pl.ds(a, n)
        lo, size = OFFS[q], 2 * HALF[q]
        group = 1024 // size

        def piece(i, j):
            zz = i * (group // 2) + j // 2
            cols = []
            for half in (0, 1):
                s, e = max(lo, half * COLS), min(lo + size, (half + 1) * COLS)
                if s < e:
                    cols.append(buf[zz, 2 * (j % 2) + half, rows, s - half * COLS : e - half * COLS])
            return cols

        def step(i, _):
            lhs = jnp.concatenate([v for j in range(group) for v in piece(i, j)], axis=1)
            rhs = panel[pl.ds(group * i, group), pl.ds(lo, size), :].reshape(1024, COLS)
            acc[rows, :] += jnp.dot(lhs, rhs, preferred_element_type=F32)
            return 0

        if q == 0:
            acc[rows, :] = jnp.zeros((n, COLS), F32)
        if NR == group:
            step(0, 0)
        else:
            lax.fori_loop(0, NR // group, step, 0)

    def begin():
        for i in range(6):
            for j in range(3):
                row, col = r * 6 + i, c * 3 + j
                inside = jnp.abs(row - col) <= jnp.maximum(band[row], band[col])
                mask[pl.ds(i * BLK, BLK), pl.ds(j * BLK, BLK)] = jnp.full((BLK, BLK), jnp.where(inside, 1.0, 0.0), F32)
        start = (ham[...].astype(F32) * mask[...]).astype(BF16)
        rs[r] = start
        ls[z, y] = start
        mine[...] = jnp.zeros((8, BLK), F32)
        terms[...] = jnp.zeros((8, COLS), F32)
        pl.semaphore_wait(barrier, NR + NC - 2)

    def prepare():
        line = lax.broadcasted_iota(jnp.int32, (8, BLK), 0)
        for f in (0, 1):
            for k in range(NC):
                tile = jnp.zeros((8, BLK), F32)
                for m in range(3):
                    tile = jnp.where(line == m, jnp.where(frag[3 * k + m] == 2 * c + f, 1.0, 0.0), tile)
                weights[f, k] = tile

    def square_rows(p):
        a, n = OFFS[p], 2 * HALF[p]
        whole(ls, rs, a, n)
        rq[r, pl.ds(a, n), :] = (acc[pl.ds(a, n), :] * mask[pl.ds(a, n), :]).astype(BF16)

    def density_rows(p):
        a, n = OFFS[p], 2 * HALF[p]
        rows = pl.ds(a, n)
        sign = 1.5 * rs[r, rows, :].astype(F32) - 0.5 * acc[rows, :]
        sign = (mask[rows, :] * sign).astype(BF16)
        n_out[rows, :] = sign
        line = r * ROWS + a + lax.broadcasted_iota(jnp.int32, (n, COLS), 0)
        column = c * COLS + lax.broadcasted_iota(jnp.int32, (n, COLS), 1)
        identity = jnp.where(line == column, 1.0, 0.0)
        density = (0.5 * (identity - sign.astype(F32))).astype(BF16)
        rd[r, rows, :] = density
        ld[z, y, rows, :] = density

    def weighted_rows(u):
        rows = pl.ds(256 * u, 256)
        rw[r, rows, :] = (acc[rows, :] * mask[rows, :]).astype(BF16)

    def energy_rows(p):
        a, n = OFFS[p], 2 * HALF[p]
        rows = pl.ds(a, n)
        energy = (acc[rows, :] * mask[rows, :]).astype(BF16)
        e_out[rows, :] = energy
        product = energy.astype(F32) * deriv[rows, :].astype(F32)
        terms[...] += jnp.sum(product.reshape(n // 8, 8, COLS), axis=0)

    def finish():
        total = jnp.sum(terms[...], axis=0, keepdims=True)
        for m in range(3):
            mine[pl.ds(m, 1), :] = total[:, m * BLK : (m + 1) * BLK]
        by_row[r] = mine[...]
        first = []
        for k in range(1, NR):
            copy = pltpu.make_async_remote_copy(
                src_ref=mine, dst_ref=by_row.at[r], send_sem=t_send.at[k - 1], recv_sem=t_recv.at[k - 1],
                device_id=(lax.rem(r + k, NR), c), device_id_type=MESH,
            )
            copy.start()
            first.append(copy)
        for copy in first:
            copy.wait_recv()
        by_col[c] = jnp.sum(by_row[...], axis=0)
        second = []
        for k in range(1, NC):
            copy = pltpu.make_async_remote_copy(
                src_ref=by_col.at[c], dst_ref=by_col.at[c], send_sem=t_send.at[6 + k], recv_sem=t_recv.at[6 + k],
                device_id=(r, lax.rem(c + k, NC)), device_id_type=MESH,
            )
            copy.start()
            second.append(copy)
        for copy in second:
            copy.wait_recv()
        for f in (0, 1):
            picked = jnp.sum(weights[f] * by_col[...], axis=0)
            pulay[pl.ds(f, 1), :] = jnp.sum(picked, axis=0, keepdims=True)
        for copy in sent + first + second:
            copy.wait_send()

    begin()
    for name in ORDER:
        digits = [int(d) for d in name if d.isdigit()]
        if name[0] == "L":
            left_step(name[1], name[2], digits[0])
        elif name[0] == "R":
            right_step(name[1], name[2], digits[0])
        elif name[:2] == "P1":
            square_rows(digits[1])
        elif name[:2] in ("P2", "P3", "P4"):
            buf, panel = {"P2": (ls, rq), "P3": (ls, rd), "P4": (ld, rw)}[name[:2]]
            if len(digits) == 2:
                whole(buf, panel, OFFS[digits[1]], 2 * HALF[digits[1]])
            else:
                part(buf, panel, 256 * digits[1], 256, digits[2])
        elif name[0] == "N":
            density_rows(digits[0])
        elif name[0] == "W":
            weighted_rows(digits[0])
        elif name[0] == "E":
            energy_rows(digits[0])
        else:
            prepare()
    finish()


def step(ham, deriv, band, frag_of):
    vmem = pl.BlockSpec(memory_space=pltpu.VMEM)
    smem = pl.BlockSpec(memory_space=pltpu.SMEM)
    dma = pltpu.SemaphoreType.DMA
    panel = pltpu.VMEM((NR, ROWS, COLS), BF16)
    slab = pltpu.VMEM((4, 4, ROWS, COLS), BF16)
    return pl.pallas_call(
        kernel,
        out_shape=(
            jax.ShapeDtypeStruct((ROWS, COLS), BF16),
            jax.ShapeDtypeStruct((ROWS, COLS), BF16),
            jax.ShapeDtypeStruct((2, BLK), F32),
        ),
        in_specs=[smem, smem, vmem, vmem],
        out_specs=(vmem, vmem, vmem),
        scratch_shapes=[
            slab, slab, panel, panel, panel, panel,
            pltpu.VMEM((ROWS, COLS), F32),
            pltpu.VMEM((ROWS, COLS), F32),
            pltpu.VMEM((8, COLS), F32),
            pltpu.VMEM((8, BLK), F32),
            pltpu.VMEM((NR, 8, BLK), F32),
            pltpu.VMEM((NC, 8, BLK), F32),
            pltpu.VMEM((2, NC, 8, BLK), F32),
            dma((128,)), dma((128,)), dma((128,)), dma((128,)), dma((22,)), dma((22,)),
        ],
        compiler_params=pltpu.CompilerParams(collective_id=0, has_side_effects=True, vmem_limit_bytes=60 << 20),
        name="sign_step",
    )(band, frag_of, ham, deriv)


def solution(mesh):
    return jax.shard_map(
        step,
        mesh=mesh,
        in_specs=(P("row", "col"), P("row", "col"), P(), P()),
        out_specs=(P("row", "col"), P("row", "col"), P("col", None)),
        check_vma=False,
    )
```

time: 433 us -> 149 us (0.34)
  waiting for transfers between devices: 309 us -> 0 us
  Pallas kernels: 0 us -> 145 us
  blocking collectives: 65.7 us -> 0 us
  matrix products: 39.3 us -> 0 us
  between operations: 14.2 us -> 0.65 us
    all_gather x6 -> x0, waiting for transfers between devices: 307 us -> none  [the longest x2 167 us: folded_product(): lax.all_gather(left_matrix, 'col', axis=1, tiled=True)]
    pallas_call x0 -> x1, Pallas kernels: none -> 145 us  [step(): pl.pallas_call(kernel, out_shape=(jax.ShapeDtypeStruct((ROWS, COLS), BF16...]
    psum x1 -> x0, blocking collectives: 65.7 us -> none  [body(): grand_total = lax.psum(partial_value, ('row', 'col'))]
    dot_general x5 -> x0, matrix products: 39.3 us -> none  [the longest x4 39.1 us: folded_product(): jnp.dot(lax.all_gather(left_matrix, 'col', axis=1, tiled=True), whole_pan...]
  transfers between devices with their start and end apart: 6 -> 0, of which waited for: 6 -> 0; matrix products, arithmetic and copies ran while one was open for 0% -> 0% of each run, Pallas kernels for 0% -> 0%
where the time goes in v1:
time: 149 us
  Pallas kernels  145 us (97%)
  local copies, waits for them, and re-layouts  3.38 us (2%)
    pallas_call x1, Pallas kernels, step(): pl.pallas_call(kernel, out_shape=(jax.ShapeDtypeStruct((ROWS, COLS), BF16...  145 us
    unnamed x7, local copies, waits for them, and re-layouts  3.38 us

profile of v1, /device:TPU:1, one launch (start us, length us, event | category | flops | bytes accessed | tf_op | source)
XLA Modules:
  0.0 148.9 jit_solution(9705305112200480268)
XLA Ops:
  0.6 144.8 %sign_step.1 = (bf16[768,384]{1,0:T(8,128)(2,1)}, bf16[768,384]{1,0:T(8,128)(2,1)}, f32[2,128]{1,0:T(2,128)}) custom-call(s32[48]{0:T(128)} %band.1, s32[48]{0:T(128)} %frag.1, bf16[768,384]{1,0:T(8,128)(2,1)} %ham.1, bf16[768,384]{1,0:T(8,128)(2,1)} %deriv.1), custom_call_target="tpu_custom_call" | custom-call | tf_op jit(solution)/shard_map/sign_step/pallas_call | solution.py:292
  145.5 0.0 copy-start
  145.5 2.0 %copy.10 = bf16[768,384]{1,0:T(8,128)(2,1)} copy(bf16[768,384]{1,0:T(8,128)(2,1)} %get-tuple-element.6) | data formatting | bytes 1179648
  147.5 0.0 copy-done
  147.5 0.0 copy-start.1
  147.5 0.8 copy.11
  148.3 0.0 copy-done.1
  148.3 0.6 copy.12
Async XLA Ops:
  145.5 2.0 %copy-start = (bf16[768,384]{1,0:T(8,128)(2,1)S(1)}, bf16[768,384]{1,0:T(8,128)(2,1)}, u32[]{:S(2)}) copy-start(bf16[768,384]{1,0:T(8,128)(2,1)} %get-tuple-element.7) | copy-start | bytes 1769476
  147.5 0.8 copy-start.1

commit v2 on v1

v2 whole, which is shorter than its diff:
```python
import functools

import jax
import jax.numpy as jnp
from jax import lax
from jax.experimental import pallas as pl
from jax.experimental.pallas import tpu as pltpu
from jax.sharding import PartitionSpec as P

MESH = pl.DeviceIdType.MESH
BLK = 128
ROWS = 768
COLS = 384
NR = 8
NC = 16
F32 = jnp.float32
BF16 = jnp.bfloat16
OFFS = (0, 256, 512, 640)
HALF = (128, 128, 64, 64)
NP = len(HALF)
LAST = NP - 1
PART = ((0, 256), (256, 256), (512, 128), (640, 128))
ORDER = (
    "LaS0", "LaS1", "prep", "RaS0", "RaS1", "RaS2", "LbS0", "RbS0", "RbS1", "LcS0", "LbS1", "RbS2",
    "RcS0", "RdS0", "RcS1", "RaS3", "LdS0", "RcS2", "RdS1", "LcS1", "LaS2", "LaS3", "RdS2", "RbS3",
    "RcS3", "RdS3", "LeS0", "P1_0", "LdS1", "RaQ0", "LbS2", "LbS3", "RbQ0", "LeS1", "P1_1", "LcS2",
    "RcQ0", "RaQ1", "LcS3", "RdQ0", "P2_00", "P2_10", "LdS2", "LdS3", "P1e_3", "RbQ1", "LeS2", "P1_2",
    "RaQ2", "LeS3", "P1_3", "RaQ3", "RcQ1", "P2_20", "RdQ1", "P2_21", "P2_11", "RbQ2", "P2_01", "RbQ3",
    "RcQ2", "RdQ2", "P2_12", "RcQ3", "P2_22", "P2_02", "RdQ3", "P2_13", "N1", "RaD1", "LaD1", "P2_03",
    "N0", "LaD0", "RaD0", "P2_23", "N2", "RaD2", "N3", "LaD3", "RaD3", "RbD1", "RbD0", "LbD0",
    "RbD2", "LcD0", "LbD1", "RbD3", "RcD1", "RdD1", "RcD0", "RcD2", "LdD0", "RdD0", "P3_00", "RcD3",
    "P3_01", "RdD2", "P3_02", "RdD3", "P3_03", "W0", "RaW0", "P3_10", "P3_11", "P3_12", "P3_13", "W1",
    "RaW1", "LcD1", "LaD2", "P3_20", "P3_21", "P3_22", "P3_23", "W2", "RbW0", "LeD0", "LdD1", "RbW1",
    "RaW2", "RaW3", "LbD2", "LbD3", "RcW0", "RdW0", "P4_00", "RcW1", "LeD1", "P4_10", "LcD2", "RdW1",
    "P4_01", "P4_11", "LcD3", "RbW2", "RbW3", "RcW2", "LdD2", "RcW3", "LdD3", "RdW2", "P4_02", "P4_12",
    "RdW3", "P4_03", "E0", "P4_13", "P4e_3", "LeD2", "P4_2", "E2", "LeD3", "P4_3", "E3", "E1",
)
FIRST = next(int(name[1]) for name in ORDER if name[0] == "E")


def kernel(band, frag, ham, deriv, n_out, e_out, pulay, ls, ld, rs, rq, rd, rw, mask, acc, terms, mine, by_row, by_col,
           weights, fetched, l_send, l_recv, r_send, r_recv, t_send, t_recv, i_sem):
    r = lax.axis_index("row")
    c = lax.axis_index("col")
    z = lax.div(c, 4)
    y = lax.rem(c, 4)
    up = {"y": lax.rem(y + 1, 4), "z": lax.rem(z + 1, 4)}
    down = {"y": lax.rem(y + 3, 4), "z": lax.rem(z + 3, 4)}
    to = {
        ("y", 0): (r, z * 4 + up["y"]),
        ("y", 1): (r, z * 4 + down["y"]),
        ("z", 0): (r, up["z"] * 4 + y),
        ("z", 1): (r, down["z"] * 4 + y),
        ("x", 0): (lax.rem(r + 2, NR), c),
        ("x", 1): (lax.rem(r + 6, NR), c),
        "core": (r + 1 - 2 * lax.rem(r, 2), c),
    }
    r_up, r_down, r_far = lax.rem(r + 2, NR), lax.rem(r + 6, NR), lax.rem(r + 4, NR)

    barrier = pltpu.get_barrier_semaphore()
    for target in to.values():
        pl.semaphore_signal(barrier, inc=1, device_id=target, device_id_type=MESH)

    def drain(ref, sem):
        pltpu.make_async_copy(ref, ref, sem).wait()

    def send(ref, target, send_sem, recv_sem):
        pltpu.make_async_remote_copy(
            src_ref=ref, dst_ref=ref, send_sem=send_sem, recv_sem=recv_sem, device_id=target, device_id_type=MESH
        ).start()

    left = {"S": ls, "D": ld}
    right = {"S": rs, "Q": rq, "D": rd, "W": rw}

    def left_step(stage, x, p):
        buf, h, a = left[x], HALF[p], OFFS[p]
        n = "SD".index(x) * NP + p
        out = l_send.at[n]
        both = pl.ds(a, 2 * h)
        one, two = pl.ds(a, h), pl.ds(a + h, h)
        ones = (pl.ds(a, h // 2), pl.ds(a + h // 2, h // 2))
        twos = (pl.ds(a + h, h // 2), pl.ds(a + h + h // 2, h // 2))
        backs = (down, up)
        far_y, far_z = lax.rem(y + 2, 4), lax.rem(z + 2, 4)
        if stage == "a":
            for axis in "yz":
                for side in (0, 1):
                    send(buf.at[z, y, both], to[axis, side], out, l_recv.at[4 * n])
        elif stage == "b":
            drain(buf.at[0, :, both], l_recv.at[4 * n])
            for side in (0, 1):
                send(buf.at[z, backs[side]["y"], ones[side]], to["y", side], out, l_recv.at[4 * n + 1])
                send(buf.at[backs[side]["z"], y, twos[side]], to["z", side], out, l_recv.at[4 * n + 1])
            for back in backs:
                for side in (0, 1):
                    send(buf.at[z, back["y"], one], to["z", side], out, l_recv.at[4 * n + 2])
                    send(buf.at[back["z"], y, two], to["y", side], out, l_recv.at[4 * n + 2])
        elif stage == "c":
            drain(buf.at[0, 0, both], l_recv.at[4 * n + 1])
            for side in (0, 1):
                send(buf.at[z, far_y, one], to["z", side], out, l_recv.at[4 * n + 2])
                send(buf.at[far_z, y, two], to["y", side], out, l_recv.at[4 * n + 2])
        elif stage == "d":
            drain(buf.at[pl.ds(0, 3), :, one], l_recv.at[4 * n + 2])
            for side in (0, 1):
                send(buf.at[backs[side]["z"], :, ones[side]], to["z", side], out, l_recv.at[4 * n + 3])
                send(buf.at[:, backs[side]["y"], twos[side]], to["y", side], out, l_recv.at[4 * n + 3])
        else:
            drain(buf.at[0, :, both], l_recv.at[4 * n + 3])

    def right_step(stage, x, p):
        buf, a, n = right[x], OFFS[p], 2 * HALF[p]
        k = "SQDW".index(x) * NP + p
        out, near, far, core = r_send.at[k], r_recv.at[3 * k], r_recv.at[3 * k + 1], r_recv.at[3 * k + 2]
        rows = pl.ds(a, n)
        if stage == "a":
            send(buf.at[r, rows], to["x", 0], out, near)
            send(buf.at[r, rows], to["x", 1], out, near)
            send(buf.at[r, rows], to["core"], out, core)
        elif stage == "b":
            drain(buf.at[pl.ds(0, 2), rows], near)
            send(buf.at[r_down, pl.ds(a, n // 2)], to["x", 0], out, far)
            send(buf.at[r_up, pl.ds(a + n // 2, n // 2)], to["x", 1], out, far)
            send(buf.at[r_down, rows], to["core"], out, core)
            send(buf.at[r_up, rows], to["core"], out, core)
        elif stage == "c":
            drain(buf.at[0, rows], far)
            send(buf.at[r_far, rows], to["core"], out, core)
        else:
            drain(buf.at[pl.ds(0, 4), rows], core)

    def all_sent():
        for n in range(2 * NP):
            drain(ls.at[pl.ds(0, 3), pl.ds(0, 2), pl.ds(0, 5 * HALF[n % NP])], l_send.at[n])
        for k in range(4 * NP):
            drain(rs.at[pl.ds(0, 7), pl.ds(0, 2 * HALF[k % NP])], r_send.at[k])

    def whole(buf, panel, a, n):
        rows = pl.ds(a, n)
        acc[rows, :] = jnp.zeros((n, COLS), F32)

        def step(i, _):
            lhs = jnp.concatenate([buf[i, j, rows, :] for j in range(4)], axis=1)
            rhs = panel[pl.ds(2 * i, 2)].reshape(4 * COLS, COLS)
            acc[rows, :] += jnp.dot(lhs, rhs, preferred_element_type=F32)
            return 0

        lax.fori_loop(0, 4, step, 0)

    def part(buf, panel, a, n, q):
        rows = pl.ds(a, n)
        lo, size = PART[q]
        group = 1024 // size

        def piece(i, j):
            zz = i * (group // 2) + j // 2
            cols = []
            for half in (0, 1):
                s, e = max(lo, half * COLS), min(lo + size, (half + 1) * COLS)
                if s < e:
                    cols.append(buf[zz, 2 * (j % 2) + half, rows, s - half * COLS : e - half * COLS])
            return cols

        def step(i, _):
            lhs = jnp.concatenate([v for j in range(group) for v in piece(i, j)], axis=1)
            rhs = panel[pl.ds(group * i, group), pl.ds(lo, size), :].reshape(1024, COLS)
            acc[rows, :] += jnp.dot(lhs, rhs, preferred_element_type=F32)
            return 0

        if q == 0:
            acc[rows, :] = jnp.zeros((n, COLS), F32)
        if NR == group:
            step(0, 0)
        else:
            lax.fori_loop(0, NR // group, step, 0)

    def fetch(i):
        return pltpu.make_async_copy((ham, deriv)[i], fetched.at[i], i_sem.at[i])

    def split(buf, panel, early):
        h = HALF[LAST]
        one, two = pl.ds(OFFS[LAST], h), pl.ds(OFFS[LAST] + h, h)
        if early:
            acc[pl.ds(OFFS[LAST], 2 * h), :] = jnp.zeros((2 * h, COLS), F32)

        def step(i, _):
            zz = lax.rem(z + i + lax.div(i, 2), 4) if early else lax.rem(z + 2, 4)
            yy = lax.rem(y + i + lax.div(i, 2), 4) if early else lax.rem(y + 2, 4)
            lhs = jnp.concatenate([buf[zz, j, one, :] for j in range(4)], axis=1)
            rhs = panel[pl.ds(2 * zz, 2)].reshape(4 * COLS, COLS)
            acc[one, :] += jnp.dot(lhs, rhs, preferred_element_type=F32)
            lhs = jnp.concatenate([buf[j, yy, two, :] for j in range(4)], axis=1)
            rows = pl.ds(pl.multiple_of(lax.rem(yy, 2) * COLS, COLS), COLS)
            rhs = jnp.concatenate([panel[2 * j + lax.div(yy, 2), rows, :] for j in range(4)], axis=0)
            acc[two, :] += jnp.dot(lhs, rhs, preferred_element_type=F32)
            return 0

        if early:
            lax.fori_loop(0, 3, step, 0)
        else:
            step(0, 0)

    def begin():
        get_ham = fetch(0)
        get_ham.start()
        fetch(1).start()
        for i in range(6):
            for j in range(3):
                row, col = r * 6 + i, c * 3 + j
                inside = jnp.abs(row - col) <= jnp.maximum(band[row], band[col])
                mask[pl.ds(i * BLK, BLK), pl.ds(j * BLK, BLK)] = jnp.full((BLK, BLK), jnp.where(inside, 1.0, 0.0), F32)
        get_ham.wait()
        start = (fetched[0].astype(F32) * mask[...]).astype(BF16)
        rs[r] = start
        ls[z, y] = start
        mine[...] = jnp.zeros((8, BLK), F32)
        terms[...] = jnp.zeros((8, COLS), F32)
        pl.semaphore_wait(barrier, len(to))

    def prepare():
        line = lax.broadcasted_iota(jnp.int32, (8, BLK), 0)
        for f in (0, 1):
            for k in range(NC):
                tile = jnp.zeros((8, BLK), F32)
                for m in range(3):
                    tile = jnp.where(line == m, jnp.where(frag[3 * k + m] == 2 * c + f, 1.0, 0.0), tile)
                weights[f, k] = tile

    def square_rows(p):
        a, n = OFFS[p], 2 * HALF[p]
        if p == LAST:
            split(ls, rs, False)
        else:
            whole(ls, rs, a, n)
        rq[r, pl.ds(a, n), :] = (acc[pl.ds(a, n), :] * mask[pl.ds(a, n), :]).astype(BF16)

    def density_rows(p):
        a, n = OFFS[p], 2 * HALF[p]
        rows = pl.ds(a, n)
        sign = 1.5 * rs[r, rows, :].astype(F32) - 0.5 * acc[rows, :]
        sign = (mask[rows, :] * sign).astype(BF16)
        n_out[rows, :] = sign
        line = r * ROWS + a + lax.broadcasted_iota(jnp.int32, (n, COLS), 0)
        column = c * COLS + lax.broadcasted_iota(jnp.int32, (n, COLS), 1)
        identity = jnp.where(line == column, 1.0, 0.0)
        density = (0.5 * (identity - sign.astype(F32))).astype(BF16)
        rd[r, rows, :] = density
        ld[z, y, rows, :] = density

    def weighted_rows(u):
        rows = pl.ds(256 * u, 256)
        rw[r, rows, :] = (acc[rows, :] * mask[rows, :]).astype(BF16)

    def energy_rows(p):
        a, n = OFFS[p], 2 * HALF[p]
        rows = pl.ds(a, n)
        if p == FIRST:
            fetch(1).wait()
        energy = (acc[rows, :] * mask[rows, :]).astype(BF16)
        e_out[rows, :] = energy
        product = energy.astype(F32) * fetched[1, rows, :].astype(F32)
        terms[...] += jnp.sum(product.reshape(n // 8, 8, COLS), axis=0)

    def finish():
        total = jnp.sum(terms[...], axis=0, keepdims=True)
        for m in range(3):
            mine[pl.ds(m, 1), :] = total[:, m * BLK : (m + 1) * BLK]
        by_row[r] = mine[...]
        for k in range(1, NR):
            pltpu.make_async_remote_copy(
                src_ref=mine, dst_ref=by_row.at[r], send_sem=t_send.at[0], recv_sem=t_recv.at[0],
                device_id=(lax.rem(r + k, NR), c), device_id_type=MESH,
            ).start()
        drain(by_row.at[pl.ds(0, NR - 1)], t_recv.at[0])
        by_col[c] = jnp.sum(by_row[...], axis=0)
        for k in range(1, NC):
            send(by_col.at[c], (r, lax.rem(c + k, NC)), t_send.at[1], t_recv.at[1])
        all_sent()
        drain(by_row.at[pl.ds(0, NR - 1)], t_send.at[0])
        drain(by_col.at[pl.ds(0, NC - 1)], t_recv.at[1])
        for f in (0, 1):
            picked = jnp.sum(weights[f] * by_col[...], axis=0)
            pulay[pl.ds(f, 1), :] = jnp.sum(picked, axis=0, keepdims=True)
        drain(by_col.at[pl.ds(0, NC - 1)], t_send.at[1])

    begin()
    for name in ORDER:
        digits = [int(d) for d in name if d.isdigit()]
        if name[0] == "L":
            left_step(name[1], name[2], digits[0])
        elif name[0] == "R":
            right_step(name[1], name[2], digits[0])
        elif name[:3] in ("P1e", "P4e"):
            split(*((ls, rs) if name[1] == "1" else (ld, rw)), True)
        elif name[:2] == "P1":
            square_rows(digits[1])
        elif name[:2] in ("P2", "P3"):
            part(ls, rq if name[1] == "2" else rd, 256 * digits[1], 256, digits[2])
        elif name[:2] == "P4":
            p = digits[1]
            if len(digits) == 3:
                part(ld, rw, OFFS[p], 2 * HALF[p], digits[2])
            elif p == LAST:
                split(ld, rw, False)
            else:
                whole(ld, rw, OFFS[p], 2 * HALF[p])
        elif name[0] == "N":
            density_rows(digits[0])
        elif name[0] == "W":
            weighted_rows(digits[0])
        elif name[0] == "E":
            energy_rows(digits[0])
        else:
            prepare()
    finish()


def write_out(n_in, e_in, p_in, n_out, e_out, p_out, sems):
    copies = [
        pltpu.make_async_copy(src, dst, sems.at[i])
        for i, (src, dst) in enumerate(((n_in, n_out), (e_in, e_out), (p_in, p_out)))
    ]
    for copy in copies:
        copy.start()
    for copy in copies:
        copy.wait()


def step(ham, deriv, band, frag_of):
    vmem = pl.BlockSpec(memory_space=pltpu.VMEM)
    smem = pl.BlockSpec(memory_space=pltpu.SMEM)
    hbm = pl.BlockSpec(memory_space=pl.ANY)
    dma = pltpu.SemaphoreType.DMA
    panel = pltpu.VMEM((NR, ROWS, COLS), BF16)
    slab = pltpu.VMEM((4, 4, ROWS, COLS), BF16)
    shapes = (((ROWS, COLS), BF16), ((ROWS, COLS), BF16), ((2, BLK), F32))
    held = pl.pallas_call(
        kernel,
        out_shape=tuple(pltpu.VMEM(*shape) for shape in shapes),
        in_specs=[smem, smem, hbm, hbm],
        out_specs=(vmem, vmem, vmem),
        scratch_shapes=[
            slab, slab, panel, panel, panel, panel,
            pltpu.VMEM((ROWS, COLS), F32),
            pltpu.VMEM((ROWS, COLS), F32),
            pltpu.VMEM((8, COLS), F32),
            pltpu.VMEM((8, BLK), F32),
            pltpu.VMEM((NR, 8, BLK), F32),
            pltpu.VMEM((NC, 8, BLK), F32),
            pltpu.VMEM((2, NC, 8, BLK), F32),
            pltpu.VMEM((2, ROWS, COLS), BF16),
            dma((2 * NP,)), dma((8 * NP,)), dma((4 * NP,)), dma((12 * NP,)), dma((2,)), dma((2,)), dma((2,)),
        ],
        compiler_params=pltpu.CompilerParams(collective_id=0, has_side_effects=True, vmem_limit_bytes=56 << 20),
        name="sign_step",
    )(band, frag_of, ham, deriv)
    return pl.pallas_call(
        write_out,
        out_shape=tuple(jax.ShapeDtypeStruct(*shape) for shape in shapes),
        in_specs=[vmem, vmem, vmem],
        out_specs=(hbm, hbm, hbm),
        scratch_shapes=[dma((3,))],
        name="write_out",
    )(*(pltpu.with_memory_space_constraint(x, pltpu.VMEM) for x in held))


def solution(mesh):
    return jax.shard_map(
        step,
        mesh=mesh,
        in_specs=(P("row", "col"), P("row", "col"), P(), P()),
        out_specs=(P("row", "col"), P("row", "col"), P("col", None)),
        check_vma=False,
    )
```

time: 149 us -> 138 us (0.926)
  Pallas kernels: 145 us -> 137 us
  local copies, waits for them, and re-layouts: 3.38 us -> 0 us
    pallas_call x1 -> x2, Pallas kernels: 145 us -> 137 us  [the longest x1 136 us: step(): pl.pallas_call(kernel, out_shape=tuple((pltpu.VMEM(*shape) for shape in s...]
    unnamed x7 -> x0, local copies, waits for them, and re-layouts: 3.38 us -> none
where the time goes in v2:
time: 138 us
  Pallas kernels  137 us (99%)
    pallas_call x1, Pallas kernels, step(): pl.pallas_call(kernel, out_shape=tuple((pltpu.VMEM(*shape) for shape in s...  136 us

profile of v2, /device:TPU:1, one launch (start us, length us, event | category | flops | bytes accessed | tf_op | source)
XLA Modules:
  0.0 137.6 jit_solution(5221668879551176958)
XLA Ops:
  0.6 135.8 %sign_step.1 = (bf16[768,384]{1,0:T(8,128)(2,1)S(1)}, bf16[768,384]{1,0:T(8,128)(2,1)S(1)}, f32[2,128]{1,0:T(2,128)S(1)}) custom-call(s32[48]{0:T(128)} %band.1, s32[48]{0:T(128)} %frag.1, bf16[768,384]{1,0:T(8,128)(2,1)} %ham.1, bf16[768,384]{1,0:T(8,128)(2,1)} %deriv.1), custom_call_target="tpu_custom_call" | custom-call | tf_op jit(solution)/shard_map/sign_step/pallas_call | solution.py:337
  136.4 1.0 write_out.1

commit v3 on v2

--- a/solution.py
+++ b/solution.py
@@ -21,19 +21,20 @@
 LAST = NP - 1
 PART = ((0, 256), (256, 256), (512, 128), (640, 128))
 ORDER = (
-    "LaS0", "LaS1", "prep", "RaS0", "RaS1", "RaS2", "LbS0", "RbS0", "RbS1", "LcS0", "LbS1", "RbS2",
-    "RcS0", "RdS0", "RcS1", "RaS3", "LdS0", "RcS2", "RdS1", "LcS1", "LaS2", "LaS3", "RdS2", "RbS3",
-    "RcS3", "RdS3", "LeS0", "P1_0", "LdS1", "RaQ0", "LbS2", "LbS3", "RbQ0", "LeS1", "P1_1", "LcS2",
-    "RcQ0", "RaQ1", "LcS3", "RdQ0", "P2_00", "P2_10", "LdS2", "LdS3", "P1e_3", "RbQ1", "LeS2", "P1_2",
-    "RaQ2", "LeS3", "P1_3", "RaQ3", "RcQ1", "P2_20", "RdQ1", "P2_21", "P2_11", "RbQ2", "P2_01", "RbQ3",
-    "RcQ2", "RdQ2", "P2_12", "RcQ3", "P2_22", "P2_02", "RdQ3", "P2_13", "N1", "RaD1", "LaD1", "P2_03",
-    "N0", "LaD0", "RaD0", "P2_23", "N2", "RaD2", "N3", "LaD3", "RaD3", "RbD1", "RbD0", "LbD0",
-    "RbD2", "LcD0", "LbD1", "RbD3", "RcD1", "RdD1", "RcD0", "RcD2", "LdD0", "RdD0", "P3_00", "RcD3",
-    "P3_01", "RdD2", "P3_02", "RdD3", "P3_03", "W0", "RaW0", "P3_10", "P3_11", "P3_12", "P3_13", "W1",
-    "RaW1", "LcD1", "LaD2", "P3_20", "P3_21", "P3_22", "P3_23", "W2", "RbW0", "LeD0", "LdD1", "RbW1",
-    "RaW2", "RaW3", "LbD2", "LbD3", "RcW0", "RdW0", "P4_00", "RcW1", "LeD1", "P4_10", "LcD2", "RdW1",
-    "P4_01", "P4_11", "LcD3", "RbW2", "RbW3", "RcW2", "LdD2", "RcW3", "LdD3", "RdW2", "P4_02", "P4_12",
-    "RdW3", "P4_03", "E0", "P4_13", "P4e_3", "LeD2", "P4_2", "E2", "LeD3", "P4_3", "E3", "E1",
+    "RaS0", "LaS1", "LaS0", "prep", "RaS1", "RbS0", "LbS1", "LxS1", "RbS1", "LbS0", "LxS0", "LcS1",
+    "RcS0", "RdS0", "RcS1", "RaS2", "RdS1", "LcS0", "LaS2", "RbS2", "RcS2", "RaS3", "RdS2", "LdS1",
+    "LdS0", "LaS3", "RbS3", "LbS2", "LxS2", "RcS3", "RdS3", "LeS1", "P1_1", "RaQ1", "LeS0", "P1_0",
+    "RaQ0", "LbS3", "LcS2", "LxS3", "RbQ1", "LcS3", "LdS2", "RbQ0", "LdS3", "P1e_3", "RcQ1", "LeS2",
+    "P1_2", "RcQ0", "RaQ2", "RdQ1", "LeS3", "P1_3", "RaQ3", "RdQ0", "P2_00", "P2_01", "P2_20", "P2_21",
+    "RbQ2", "P2_10", "P2_11", "RbQ3", "RcQ2", "RdQ2", "P2_02", "P2_22", "RcQ3", "P2_12", "RdQ3", "P2_03",
+    "N0", "RaD0", "LaD0", "P2_13", "N1", "RaD1", "LaD1", "P2_23", "N2", "RaD2", "N3", "RaD3",
+    "LaD3", "RbD0", "LbD0", "LxD0", "RbD1", "LbD1", "LxD1", "RbD2", "LcD0", "RbD3", "RcD0", "RdD0",
+    "P3_20", "LcD1", "LaD2", "RcD1", "P3_00", "RcD2", "P3_10", "RdD1", "RcD3", "P3_01", "RdD2", "P3_02",
+    "RdD3", "P3_03", "W0", "RaW0", "P3_11", "P3_12", "P3_13", "W1", "RaW1", "P3_21", "P3_22", "P3_23",
+    "W2", "RaW2", "LdD0", "LdD1", "RbW0", "RaW3", "LbD2", "LbD3", "LxD2", "RbW1", "LeD0", "RbW2",
+    "RcW0", "LeD1", "LcD2", "LxD3", "RdW0", "P4_10", "LcD3", "P4_00", "RbW3", "RcW1", "LdD2", "RcW2",
+    "RdW1", "P4_01", "RdW2", "RcW3", "P4_11", "P4_12", "LdD3", "RdW3", "P4e_3", "P4_13", "E1", "LeD2",
+    "P4_2", "E2", "P4_02", "P4_03", "LeD3", "P4_3", "E3", "E0",
 )
 FIRST = next(int(name[1]) for name in ORDER if name[0] == "E")
 
@@ -74,8 +75,7 @@
 
     def left_step(stage, x, p):
         buf, h, a = left[x], HALF[p], OFFS[p]
-        n = "SD".index(x) * NP + p
-        out = l_send.at[n]
+        out = l_send.at[p]
         both = pl.ds(a, 2 * h)
         one, two = pl.ds(a, h), pl.ds(a + h, h)
         ones = (pl.ds(a, h // 2), pl.ds(a + h // 2, h // 2))
@@ -85,33 +85,34 @@
         if stage == "a":
             for axis in "yz":
                 for side in (0, 1):
-                    send(buf.at[z, y, both], to[axis, side], out, l_recv.at[4 * n])
+                    send(buf.at[z, y, both], to[axis, side], out, l_recv.at[4 * p])
         elif stage == "b":
-            drain(buf.at[0, :, both], l_recv.at[4 * n])
+            drain(buf.at[0, :, both], l_recv.at[4 * p])
             for side in (0, 1):
-                send(buf.at[z, backs[side]["y"], ones[side]], to["y", side], out, l_recv.at[4 * n + 1])
-                send(buf.at[backs[side]["z"], y, twos[side]], to["z", side], out, l_recv.at[4 * n + 1])
+                send(buf.at[z, backs[side]["y"], ones[side]], to["y", side], out, l_recv.at[4 * p + 1])
+                send(buf.at[backs[side]["z"], y, twos[side]], to["z", side], out, l_recv.at[4 * p + 1])
+        elif stage == "x":
             for back in backs:
                 for side in (0, 1):
-                    send(buf.at[z, back["y"], one], to["z", side], out, l_recv.at[4 * n + 2])
-                    send(buf.at[back["z"], y, two], to["y", side], out, l_recv.at[4 * n + 2])
+                    send(buf.at[z, back["y"], one], to["z", side], out, l_recv.at[4 * p + 2])
+                    send(buf.at[back["z"], y, two], to["y", side], out, l_recv.at[4 * p + 2])
         elif stage == "c":
-            drain(buf.at[0, 0, both], l_recv.at[4 * n + 1])
+            drain(buf.at[0, 0, both], l_recv.at[4 * p + 1])
             for side in (0, 1):
-                send(buf.at[z, far_y, one], to["z", side], out, l_recv.at[4 * n + 2])
-                send(buf.at[far_z, y, two], to["y", side], out, l_recv.at[4 * n + 2])
+                send(buf.at[z, far_y, one], to["z", side], out, l_recv.at[4 * p + 2])
+                send(buf.at[far_z, y, two], to["y", side], out, l_recv.at[4 * p + 2])
         elif stage == "d":
-            drain(buf.at[pl.ds(0, 3), :, one], l_recv.at[4 * n + 2])
+            drain(buf.at[pl.ds(0, 3), :, one], l_recv.at[4 * p + 2])
             for side in (0, 1):
-                send(buf.at[backs[side]["z"], :, ones[side]], to["z", side], out, l_recv.at[4 * n + 3])
-                send(buf.at[:, backs[side]["y"], twos[side]], to["y", side], out, l_recv.at[4 * n + 3])
-        else:
-            drain(buf.at[0, :, both], l_recv.at[4 * n + 3])
+                send(buf.at[backs[side]["z"], :, ones[side]], to["z", side], out, l_recv.at[4 * p + 3])
+                send(buf.at[:, backs[side]["y"], twos[side]], to["y", side], out, l_recv.at[4 * p + 3])
+        else:
+            drain(buf.at[0, :, both], l_recv.at[4 * p + 3])
 
     def right_step(stage, x, p):
         buf, a, n = right[x], OFFS[p], 2 * HALF[p]
-        k = "SQDW".index(x) * NP + p
-        out, near, far, core = r_send.at[k], r_recv.at[3 * k], r_recv.at[3 * k + 1], r_recv.at[3 * k + 2]
+        out, near, far = r_send.at[p], r_recv.at[p], r_recv.at[NP + p]
+        core = r_recv.at[2 * NP + 2 * p + "SQDW".index(x) % 2]
         rows = pl.ds(a, n)
         if stage == "a":
             send(buf.at[r, rows], to["x", 0], out, near)
@@ -130,10 +131,9 @@
             drain(buf.at[pl.ds(0, 4), rows], core)
 
     def all_sent():
-        for n in range(2 * NP):
-            drain(ls.at[pl.ds(0, 3), pl.ds(0, 2), pl.ds(0, 5 * HALF[n % NP])], l_send.at[n])
-        for k in range(4 * NP):
-            drain(rs.at[pl.ds(0, 7), pl.ds(0, 2 * HALF[k % NP])], r_send.at[k])
+        for p in range(NP):
+            drain(ls.at[pl.ds(0, 3), :, pl.ds(0, 5 * HALF[p])], l_send.at[p])
+            drain(ls.at[:, :, pl.ds(0, 7 * HALF[p] // 2)], r_send.at[p])
 
     def whole(buf, panel, a, n):
         rows = pl.ds(a, n)
@@ -349,7 +349,7 @@
             pltpu.VMEM((NC, 8, BLK), F32),
             pltpu.VMEM((2, NC, 8, BLK), F32),
             pltpu.VMEM((2, ROWS, COLS), BF16),
-            dma((2 * NP,)), dma((8 * NP,)), dma((4 * NP,)), dma((12 * NP,)), dma((2,)), dma((2,)), dma((2,)),
+            dma((NP,)), dma((4 * NP,)), dma((NP,)), dma((4 * NP,)), dma((2,)), dma((2,)), dma((2,)),
         ],
         compiler_params=pltpu.CompilerParams(collective_id=0, has_side_effects=True, vmem_limit_bytes=56 << 20),
         name="sign_step",

time: 138 us -> 133 us (0.964)
  Pallas kernels: 137 us -> 132 us
    pallas_call x1, Pallas kernels: 136 us -> 131 us  [step(): pl.pallas_call(kernel, out_shape=tuple((pltpu.VMEM(*shape) for shape in s...]
where the time goes in v3:
time: 133 us
  Pallas kernels  132 us (99%)
    pallas_call x1, Pallas kernels, step(): pl.pallas_call(kernel, out_shape=tuple((pltpu.VMEM(*shape) for shape in s...  131 us

profile of v3, /device:TPU:1, one launch (start us, length us, event | category | flops | bytes accessed | tf_op | source)
XLA Modules:
  0.0 133.3 jit_solution(18072254804145178740)
XLA Ops:
  0.6 131.4 %sign_step.1 = (bf16[768,384]{1,0:T(8,128)(2,1)S(1)}, bf16[768,384]{1,0:T(8,128)(2,1)S(1)}, f32[2,128]{1,0:T(2,128)S(1)}) custom-call(s32[48]{0:T(128)} %band.1, s32[48]{0:T(128)} %frag.1, bf16[768,384]{1,0:T(8,128)(2,1)} %ham.1, bf16[768,384]{1,0:T(8,128)(2,1)} %deriv.1), custom_call_target="tpu_custom_call" | custom-call | tf_op jit(solution)/shard_map/sign_step/pallas_call | solution.py:337
  132.1 1.0 write_out.1

commit v4 on v3

--- a/solution.py
+++ b/solution.py
@@ -18,29 +18,34 @@
 OFFS = (0, 256, 512, 640)
 HALF = (128, 128, 64, 64)
 NP = len(HALF)
+PIECES = ((0, 256), (256, 128), (384, 128), (512, 128), (640, 64), (704, 64))
+NS = len(PIECES)
 LAST = NP - 1
 PART = ((0, 256), (256, 256), (512, 128), (640, 128))
 ORDER = (
-    "RaS0", "LaS1", "LaS0", "prep", "RaS1", "RbS0", "LbS1", "LxS1", "RbS1", "LbS0", "LxS0", "LcS1",
-    "RcS0", "RdS0", "RcS1", "RaS2", "RdS1", "LcS0", "LaS2", "RbS2", "RcS2", "RaS3", "RdS2", "LdS1",
-    "LdS0", "LaS3", "RbS3", "LbS2", "LxS2", "RcS3", "RdS3", "LeS1", "P1_1", "RaQ1", "LeS0", "P1_0",
-    "RaQ0", "LbS3", "LcS2", "LxS3", "RbQ1", "LcS3", "LdS2", "RbQ0", "LdS3", "P1e_3", "RcQ1", "LeS2",
-    "P1_2", "RcQ0", "RaQ2", "RdQ1", "LeS3", "P1_3", "RaQ3", "RdQ0", "P2_00", "P2_01", "P2_20", "P2_21",
-    "RbQ2", "P2_10", "P2_11", "RbQ3", "RcQ2", "RdQ2", "P2_02", "P2_22", "RcQ3", "P2_12", "RdQ3", "P2_03",
-    "N0", "RaD0", "LaD0", "P2_13", "N1", "RaD1", "LaD1", "P2_23", "N2", "RaD2", "N3", "RaD3",
-    "LaD3", "RbD0", "LbD0", "LxD0", "RbD1", "LbD1", "LxD1", "RbD2", "LcD0", "RbD3", "RcD0", "RdD0",
-    "P3_20", "LcD1", "LaD2", "RcD1", "P3_00", "RcD2", "P3_10", "RdD1", "RcD3", "P3_01", "RdD2", "P3_02",
-    "RdD3", "P3_03", "W0", "RaW0", "P3_11", "P3_12", "P3_13", "W1", "RaW1", "P3_21", "P3_22", "P3_23",
-    "W2", "RaW2", "LdD0", "LdD1", "RbW0", "RaW3", "LbD2", "LbD3", "LxD2", "RbW1", "LeD0", "RbW2",
-    "RcW0", "LeD1", "LcD2", "LxD3", "RdW0", "P4_10", "LcD3", "P4_00", "RbW3", "RcW1", "LdD2", "RcW2",
-    "RdW1", "P4_01", "RdW2", "RcW3", "P4_11", "P4_12", "LdD3", "RdW3", "P4e_3", "P4_13", "E1", "LeD2",
-    "P4_2", "E2", "P4_02", "P4_03", "LeD3", "P4_3", "E3", "E0",
+    "LaS3", "RaS1", "LaS0", "prep", "RaS3", "LaS1", "RaS0", "RaS2", "RbS1", "RbS3", "LbS0", "LxS0",
+    "RbS0", "LbS1", "RbS2", "RaS5", "LcS0", "LxS1", "RcS1", "LaS2", "RcS3", "RaS4", "RdS1", "RdS3",
+    "RcS0", "RcS2", "RdS0", "LcS1", "RbS5", "RdS2", "RbS4", "LdS0", "RcS5", "RcS4", "RdS5", "RdS4",
+    "LbS2", "LdS1", "LxS2", "LbS3", "LeS0", "P1_0", "RaQ0", "LcS2", "LxS3", "LeS1", "P1_1", "RaQ1",
+    "RaQ2", "LcS3", "LdS2", "RbQ0", "RbQ1", "LdS3", "P1e_3", "RbQ2", "LeS2", "P1_2", "RaQ3", "RcQ0",
+    "LeS3", "P1_3", "RaQ5", "RaQ4", "RcQ1", "RdQ0", "P2_10", "P2_20", "RdQ1", "RcQ2", "P2_00", "RbQ3",
+    "RdQ2", "P2_01", "RbQ5", "P2_11", "RbQ4", "P2_21", "RcQ3", "RcQ5", "RdQ3", "P2_12", "RcQ4", "P2_02",
+    "RdQ5", "P2_22", "RdQ4", "P2_03", "N0", "RaD0", "LaD0", "P2_13", "N1", "RaD1", "LaD1", "RaD2",
+    "P2_23", "N2", "LaD2", "RaD3", "N3", "RaD5", "RbD0", "RaD4", "LbD0", "LxD0", "RbD1", "RbD2",
+    "LbD1", "LxD1", "RbD3", "RbD5", "LcD0", "LaD3", "RcD0", "RbD4", "RdD0", "P3_10", "RcD1", "P3_20",
+    "LcD1", "LbD2", "LxD2", "RcD2", "P3_00", "RdD1", "RcD3", "RdD2", "P3_11", "RcD4", "RcD5", "P3_21",
+    "RdD3", "P3_22", "RdD5", "RdD4", "P3_23", "W2", "RaW5", "P3_12", "P3_13", "W1", "RaW2", "P3_01",
+    "P3_02", "LdD0", "P3_03", "W0", "RaW0", "RaW1", "RaW3", "RbW5", "LbD3", "RbW2", "LdD1", "LcD2",
+    "LxD3", "RbW0", "RaW4", "RbW1", "LeD0", "RbW3", "LcD3", "RcW5", "RcW2", "RdW5", "RdW2", "RcW0",
+    "LeD1", "RbW4", "RdW0", "P4_00", "RcW1", "LdD2", "P4_10", "RcW3", "RdW1", "P4_01", "RcW4", "RdW3",
+    "P4_02", "LdD3", "P4_11", "P4_12", "RdW4", "P4e_3", "LeD2", "P4_03", "P4_13", "E1", "P4_2", "LeD3",
+    "P4_3", "E3", "E2", "E0",
 )
 FIRST = next(int(name[1]) for name in ORDER if name[0] == "E")
 
 
-def kernel(band, frag, ham, deriv, n_out, e_out, pulay, ls, ld, rs, rq, rd, rw, mask, acc, terms, mine, by_row, by_col,
-           weights, fetched, l_send, l_recv, r_send, r_recv, t_send, t_recv, i_sem):
+def kernel(band_in, frag_in, ham, deriv, n_out, e_out, pulay, ls, ld, rs, rq, rd, rw, mask, acc, terms, mine, by_row, by_col,
+           weights, fetched, band, frag, l_send, l_recv, r_send, r_recv, t_send, t_recv, i_sem):
     r = lax.axis_index("row")
     c = lax.axis_index("col")
     z = lax.div(c, 4)
@@ -83,6 +88,8 @@
         backs = (down, up)
         far_y, far_z = lax.rem(y + 2, 4), lax.rem(z + 2, 4)
         if stage == "a":
+            if x == "S":
+                start_rows(a, 2 * h)
             for axis in "yz":
                 for side in (0, 1):
                     send(buf.at[z, y, both], to[axis, side], out, l_recv.at[4 * p])
@@ -110,11 +117,14 @@
             drain(buf.at[0, :, both], l_recv.at[4 * p + 3])
 
     def right_step(stage, x, p):
-        buf, a, n = right[x], OFFS[p], 2 * HALF[p]
-        out, near, far = r_send.at[p], r_recv.at[p], r_recv.at[NP + p]
-        core = r_recv.at[2 * NP + 2 * p + "SQDW".index(x) % 2]
+        buf = right[x]
+        a, n = PIECES[p]
+        out, near, far = r_send.at[p], r_recv.at[p], r_recv.at[NS + p]
+        core = r_recv.at[2 * NS + 2 * p + "SQDW".index(x) % 2]
         rows = pl.ds(a, n)
         if stage == "a":
+            if x == "S":
+                start_rows(a, n)
             send(buf.at[r, rows], to["x", 0], out, near)
             send(buf.at[r, rows], to["x", 1], out, near)
             send(buf.at[r, rows], to["core"], out, core)
@@ -133,7 +143,8 @@
     def all_sent():
         for p in range(NP):
             drain(ls.at[pl.ds(0, 3), :, pl.ds(0, 5 * HALF[p])], l_send.at[p])
-            drain(ls.at[:, :, pl.ds(0, 7 * HALF[p] // 2)], r_send.at[p])
+        for p, (_, n) in enumerate(PIECES):
+            drain(ls.at[:, :, pl.ds(0, 7 * n // 4)], r_send.at[p])
 
     def whole(buf, panel, a, n):
         rows = pl.ds(a, n)
@@ -175,7 +186,11 @@
             lax.fori_loop(0, NR // group, step, 0)
 
     def fetch(i):
-        return pltpu.make_async_copy((ham, deriv)[i], fetched.at[i], i_sem.at[i])
+        if i < 3:
+            rows = pl.ds(256 * i, 256)
+            return pltpu.make_async_copy(ham.at[rows], fetched.at[0, rows], i_sem.at[i])
+        src, dst = ((deriv, fetched.at[1]), (band_in, band), (frag_in, frag))[i - 3]
+        return pltpu.make_async_copy(src, dst, i_sem.at[i])
 
     def split(buf, panel, early):
         h = HALF[LAST]
@@ -200,31 +215,43 @@
         else:
             step(0, 0)
 
+    first = int(ORDER[0][3])
+    first = (OFFS if ORDER[0][0] == "L" else [a for a, _ in PIECES])[first] // 256
+    order_of_rows = (first, *(i for i in range(3) if i != first))
+    ready = {}
+
+    def start_rows(a, n):
+        for i in range(a // BLK, (a + n + BLK - 1) // BLK):
+            if i in ready:
+                continue
+            if not ready:
+                fetch(4).wait()
+            if i // 2 not in ready.values():
+                fetch(i // 2).wait()
+            ready[i] = i // 2
+            rows = pl.ds(i * BLK, BLK)
+            for j in range(3):
+                row, col, cols = r * 6 + i, c * 3 + j, pl.ds(j * BLK, BLK)
+                inside = jnp.abs(row - col) <= jnp.maximum(band[row], band[col])
+                block = jnp.full((BLK, BLK), jnp.where(inside, 1.0, 0.0), F32)
+                mask[rows, cols] = block
+                start = (fetched[0, rows, cols].astype(F32) * block).astype(BF16)
+                rs[r, rows, cols] = start
+                ls[z, y, rows, cols] = start
+
     def begin():
-        get_ham = fetch(0)
-        get_ham.start()
-        fetch(1).start()
-        for i in range(6):
-            for j in range(3):
-                row, col = r * 6 + i, c * 3 + j
-                inside = jnp.abs(row - col) <= jnp.maximum(band[row], band[col])
-                mask[pl.ds(i * BLK, BLK), pl.ds(j * BLK, BLK)] = jnp.full((BLK, BLK), jnp.where(inside, 1.0, 0.0), F32)
-        get_ham.wait()
-        start = (fetched[0].astype(F32) * mask[...]).astype(BF16)
-        rs[r] = start
-        ls[z, y] = start
-        mine[...] = jnp.zeros((8, BLK), F32)
+        for i in (4, *order_of_rows, 5, 3):
+            fetch(i).start()
         terms[...] = jnp.zeros((8, COLS), F32)
+        start_rows(256 * order_of_rows[0], 256)
         pl.semaphore_wait(barrier, len(to))
 
     def prepare():
-        line = lax.broadcasted_iota(jnp.int32, (8, BLK), 0)
+        fetch(5).wait()
         for f in (0, 1):
-            for k in range(NC):
-                tile = jnp.zeros((8, BLK), F32)
-                for m in range(3):
-                    tile = jnp.where(line == m, jnp.where(frag[3 * k + m] == 2 * c + f, 1.0, 0.0), tile)
-                weights[f, k] = tile
+            for j in range(3 * NC):
+                weight = jnp.where(frag[j] == 2 * c + f, 1.0, 0.0)
+                weights[f, j // 3, :, pl.ds(j % 3 * BLK, BLK)] = jnp.full((1, BLK), weight, F32)
 
     def square_rows(p):
         a, n = OFFS[p], 2 * HALF[p]
@@ -255,16 +282,14 @@
         a, n = OFFS[p], 2 * HALF[p]
         rows = pl.ds(a, n)
         if p == FIRST:
-            fetch(1).wait()
+            fetch(3).wait()
         energy = (acc[rows, :] * mask[rows, :]).astype(BF16)
         e_out[rows, :] = energy
         product = energy.astype(F32) * fetched[1, rows, :].astype(F32)
         terms[...] += jnp.sum(product.reshape(n // 8, 8, COLS), axis=0)
 
     def finish():
-        total = jnp.sum(terms[...], axis=0, keepdims=True)
-        for m in range(3):
-            mine[pl.ds(m, 1), :] = total[:, m * BLK : (m + 1) * BLK]
+        mine[...] = jnp.sum(terms[...], axis=0, keepdims=True)
         by_row[r] = mine[...]
         for k in range(1, NR):
             pltpu.make_async_remote_copy(
@@ -280,7 +305,7 @@
         drain(by_col.at[pl.ds(0, NC - 1)], t_recv.at[1])
         for f in (0, 1):
             picked = jnp.sum(weights[f] * by_col[...], axis=0)
-            pulay[pl.ds(f, 1), :] = jnp.sum(picked, axis=0, keepdims=True)
+            pulay[pl.ds(f, 1), :] = picked[:, :BLK] + picked[:, BLK : 2 * BLK] + picked[:, 2 * BLK :]
         drain(by_col.at[pl.ds(0, NC - 1)], t_send.at[1])
 
     begin()
@@ -328,7 +353,6 @@
 
 def step(ham, deriv, band, frag_of):
     vmem = pl.BlockSpec(memory_space=pltpu.VMEM)
-    smem = pl.BlockSpec(memory_space=pltpu.SMEM)
     hbm = pl.BlockSpec(memory_space=pl.ANY)
     dma = pltpu.SemaphoreType.DMA
     panel = pltpu.VMEM((NR, ROWS, COLS), BF16)
@@ -337,19 +361,21 @@
     held = pl.pallas_call(
         kernel,
         out_shape=tuple(pltpu.VMEM(*shape) for shape in shapes),
-        in_specs=[smem, smem, hbm, hbm],
+        in_specs=[hbm, hbm, hbm, hbm],
         out_specs=(vmem, vmem, vmem),
         scratch_shapes=[
             slab, slab, panel, panel, panel, panel,
             pltpu.VMEM((ROWS, COLS), F32),
             pltpu.VMEM((ROWS, COLS), F32),
             pltpu.VMEM((8, COLS), F32),
-            pltpu.VMEM((8, BLK), F32),
-            pltpu.VMEM((NR, 8, BLK), F32),
-            pltpu.VMEM((NC, 8, BLK), F32),
-            pltpu.VMEM((2, NC, 8, BLK), F32),
+            pltpu.VMEM((1, COLS), F32),
+            pltpu.VMEM((NR, 1, COLS), F32),
+            pltpu.VMEM((NC, 1, COLS), F32),
+            pltpu.VMEM((2, NC, 1, COLS), F32),
             pltpu.VMEM((2, ROWS, COLS), BF16),
-            dma((NP,)), dma((4 * NP,)), dma((NP,)), dma((4 * NP,)), dma((2,)), dma((2,)), dma((2,)),
+            pltpu.SMEM((6 * NR,), jnp.int32),
+            pltpu.SMEM((6 * NR,), jnp.int32),
+            dma((NP,)), dma((4 * NP,)), dma((NS,)), dma((4 * NS,)), dma((2,)), dma((2,)), dma((6,)),
         ],
         compiler_params=pltpu.CompilerParams(collective_id=0, has_side_effects=True, vmem_limit_bytes=56 << 20),
         name="sign_step",

time: 133 us -> 131 us (0.985)
  Pallas kernels: 132 us -> 130 us
    pallas_call x1, Pallas kernels: 131 us -> 129 us  [step(): pl.pallas_call(kernel, out_shape=tuple((pltpu.VMEM(*shape) for shape in s...]
where the time goes in v4:
time: 131 us
  Pallas kernels  130 us (99%)
    pallas_call x1, Pallas kernels, step(): pl.pallas_call(kernel, out_shape=tuple((pltpu.VMEM(*shape) for shape in s...  129 us

profile of v4, /device:TPU:1, one launch (start us, length us, event | category | flops | bytes accessed | tf_op | source)
XLA Modules:
  0.0 130.9 jit_solution(11537326016344392088)
XLA Ops:
  0.6 129.1 %sign_step.1 = (bf16[768,384]{1,0:T(8,128)(2,1)S(1)}, bf16[768,384]{1,0:T(8,128)(2,1)S(1)}, f32[2,128]{1,0:T(2,128)S(1)}) custom-call(s32[48]{0:T(128)} %band_in.1, s32[48]{0:T(128)} %frag_in.1, bf16[768,384]{1,0:T(8,128)(2,1)} %ham.1, bf16[768,384]{1,0:T(8,128)(2,1)} %deriv.1), custom_call_target="tpu_custom_call" | custom-call | tf_op jit(solution)/shard_map/sign_step/pallas_call | solution.py:361
  129.7 1.0 write_out.1

commit v5 on v4

--- a/solution.py
+++ b/solution.py
@@ -194,26 +194,31 @@
 
     def split(buf, panel, early):
         h = HALF[LAST]
-        one, two = pl.ds(OFFS[LAST], h), pl.ds(OFFS[LAST] + h, h)
+        one, two, both = pl.ds(OFFS[LAST], h), pl.ds(OFFS[LAST] + h, h), pl.ds(OFFS[LAST], 2 * h)
+        zs, ys = (lax.rem(z + 2, 4), z, up["z"], down["z"]), (lax.rem(y + 2, 4), y, up["y"], down["y"])
+
+        def add(rows, blocks):
+            lhs = jnp.concatenate([buf[zz, yy, rows, :] for zz, yy in blocks], axis=1)
+            half = [pl.ds(pl.multiple_of(lax.rem(yy, 2) * COLS, COLS), COLS) for _, yy in blocks]
+            rhs = jnp.concatenate(
+                [panel[2 * zz + lax.div(yy, 2), part_of, :] for (zz, yy), part_of in zip(blocks, half)], axis=0
+            )
+            acc[rows, :] += jnp.dot(lhs, rhs, preferred_element_type=F32)
+
         if early:
-            acc[pl.ds(OFFS[LAST], 2 * h), :] = jnp.zeros((2 * h, COLS), F32)
-
-        def step(i, _):
-            zz = lax.rem(z + i + lax.div(i, 2), 4) if early else lax.rem(z + 2, 4)
-            yy = lax.rem(y + i + lax.div(i, 2), 4) if early else lax.rem(y + 2, 4)
-            lhs = jnp.concatenate([buf[zz, j, one, :] for j in range(4)], axis=1)
-            rhs = panel[pl.ds(2 * zz, 2)].reshape(4 * COLS, COLS)
-            acc[one, :] += jnp.dot(lhs, rhs, preferred_element_type=F32)
-            lhs = jnp.concatenate([buf[j, yy, two, :] for j in range(4)], axis=1)
-            rows = pl.ds(pl.multiple_of(lax.rem(yy, 2) * COLS, COLS), COLS)
-            rhs = jnp.concatenate([panel[2 * j + lax.div(yy, 2), rows, :] for j in range(4)], axis=0)
-            acc[two, :] += jnp.dot(lhs, rhs, preferred_element_type=F32)
-            return 0
-
-        if early:
+            acc[both, :] = jnp.zeros((2 * h, COLS), F32)
+
+            def step(i, _):
+                zz = lax.rem(z + i + lax.div(i, 2), 4)
+                add(both, [(zz, yy) for yy in ys[1:]])
+                return 0
+
             lax.fori_loop(0, 3, step, 0)
-        else:
-            step(0, 0)
+            add(one, [(zz, ys[0]) for zz in zs[1:]])
+            add(two, [(zs[0], yy) for yy in ys[1:]])
+        else:
+            add(one, [(zs[0], yy) for yy in ys])
+            add(two, [(zz, ys[0]) for zz in zs])
 
     first = int(ORDER[0][3])
     first = (OFFS if ORDER[0][0] == "L" else [a for a, _ in PIECES])[first] // 256
@@ -291,15 +296,22 @@
     def finish():
         mine[...] = jnp.sum(terms[...], axis=0, keepdims=True)
         by_row[r] = mine[...]
-        for k in range(1, NR):
-            pltpu.make_async_remote_copy(
-                src_ref=mine, dst_ref=by_row.at[r], send_sem=t_send.at[0], recv_sem=t_recv.at[0],
-                device_id=(lax.rem(r + k, NR), c), device_id_type=MESH,
-            ).start()
+        for k in (4, 2, 6, 0):
+            for other in (True, False):
+                if k == 0 and not other:
+                    continue
+                peer = lax.rem(r + k, NR)
+                peer = peer + 1 - 2 * lax.rem(r, 2) if other else peer
+                pltpu.make_async_remote_copy(
+                    src_ref=mine, dst_ref=by_row.at[r], send_sem=t_send.at[0], recv_sem=t_recv.at[0],
+                    device_id=(peer, c), device_id_type=MESH,
+                ).start()
         drain(by_row.at[pl.ds(0, NR - 1)], t_recv.at[0])
         by_col[c] = jnp.sum(by_row[...], axis=0)
-        for k in range(1, NC):
-            send(by_col.at[c], (r, lax.rem(c + k, NC)), t_send.at[1], t_recv.at[1])
+        steps = sorted(range(1, NC), key=lambda k: -min(k // 4, 4 - k // 4) - min(k % 4, 4 - k % 4))
+        for k in steps:
+            peer = lax.rem(z + k // 4, 4) * 4 + lax.rem(y + k % 4, 4)
+            send(by_col.at[c], (r, peer), t_send.at[1], t_recv.at[1])
         all_sent()
         drain(by_row.at[pl.ds(0, NR - 1)], t_send.at[0])
         drain(by_col.at[pl.ds(0, NC - 1)], t_recv.at[1])

time: 131 us -> 131 us (level)
  no operation moved by 1% of the time
where the time goes in v5:
time: 131 us
  Pallas kernels  130 us (99%)
    pallas_call x1, Pallas kernels, step(): pl.pallas_call(kernel, out_shape=tuple((pltpu.VMEM(*shape) for shape in s...  129 us

profile of v5, /device:TPU:1, one launch (start us, length us, event | category | flops | bytes accessed | tf_op | source)
XLA Modules:
  0.0 130.7 jit_solution(4120958301096036130)
XLA Ops:
  0.6 128.8 %sign_step.1 = (bf16[768,384]{1,0:T(8,128)(2,1)S(1)}, bf16[768,384]{1,0:T(8,128)(2,1)S(1)}, f32[2,128]{1,0:T(2,128)S(1)}) custom-call(s32[48]{0:T(128)} %band_in.1, s32[48]{0:T(128)} %frag_in.1, bf16[768,384]{1,0:T(8,128)(2,1)} %ham.1, bf16[768,384]{1,0:T(8,128)(2,1)} %deriv.1), custom_call_target="tpu_custom_call" | custom-call | tf_op jit(solution)/shard_map/sign_step/pallas_call | solution.py:373
  129.5 1.0 write_out.1

commit v6 on v5

--- a/solution.py
+++ b/solution.py
@@ -38,8 +38,8 @@
     "P3_02", "LdD0", "P3_03", "W0", "RaW0", "RaW1", "RaW3", "RbW5", "LbD3", "RbW2", "LdD1", "LcD2",
     "LxD3", "RbW0", "RaW4", "RbW1", "LeD0", "RbW3", "LcD3", "RcW5", "RcW2", "RdW5", "RdW2", "RcW0",
     "LeD1", "RbW4", "RdW0", "P4_00", "RcW1", "LdD2", "P4_10", "RcW3", "RdW1", "P4_01", "RcW4", "RdW3",
-    "P4_02", "LdD3", "P4_11", "P4_12", "RdW4", "P4e_3", "LeD2", "P4_03", "P4_13", "E1", "P4_2", "LeD3",
-    "P4_3", "E3", "E2", "E0",
+    "P4_02", "LdD3", "P4_11", "P4_12", "RdW4", "P4e_3", "LeD2", "P4_03", "P4_13", "E1", "E0", "P4_2", "E2",
+    "LeD3", "P4_3", "E3",
 )
 FIRST = next(int(name[1]) for name in ORDER if name[0] == "E")
 
@@ -353,10 +353,13 @@
 
 
 def write_out(n_in, e_in, p_in, n_out, e_out, p_out, sems):
-    copies = [
-        pltpu.make_async_copy(src, dst, sems.at[i])
-        for i, (src, dst) in enumerate(((n_in, n_out), (e_in, e_out), (p_in, p_out)))
+    pairs = [
+        (src.at[pl.ds(192 * i, 192)], dst.at[pl.ds(192 * i, 192)])
+        for src, dst in ((n_in, n_out), (e_in, e_out))
+        for i in range(ROWS // 192)
     ]
+    pairs.append((p_in, p_out))
+    copies = [pltpu.make_async_copy(src, dst, sems.at[i]) for i, (src, dst) in enumerate(pairs)]
     for copy in copies:
         copy.start()
     for copy in copies:
@@ -397,7 +400,7 @@
         out_shape=tuple(jax.ShapeDtypeStruct(*shape) for shape in shapes),
         in_specs=[vmem, vmem, vmem],
         out_specs=(hbm, hbm, hbm),
-        scratch_shapes=[dma((3,))],
+        scratch_shapes=[dma((9,))],
         name="write_out",
     )(*(pltpu.with_memory_space_constraint(x, pltpu.VMEM) for x in held))
 

time: 131 us -> 131 us (level)
  no operation moved by 1% of the time
where the time goes in v6:
time: 131 us
  Pallas kernels  130 us (99%)
    pallas_call x1, Pallas kernels, step(): pl.pallas_call(kernel, out_shape=tuple((pltpu.VMEM(*shape) for shape in s...  129 us

profile of v6, /device:TPU:1, one launch (start us, length us, event | category | flops | bytes accessed | tf_op | source)
XLA Modules:
  0.0 130.8 jit_solution(10838829599970114465)
XLA Ops:
  0.6 128.9 %sign_step.1 = (bf16[768,384]{1,0:T(8,128)(2,1)S(1)}, bf16[768,384]{1,0:T(8,128)(2,1)S(1)}, f32[2,128]{1,0:T(2,128)S(1)}) custom-call(s32[48]{0:T(128)} %band_in.1, s32[48]{0:T(128)} %frag_in.1, bf16[768,384]{1,0:T(8,128)(2,1)} %ham.1, bf16[768,384]{1,0:T(8,128)(2,1)} %deriv.1), custom_call_target="tpu_custom_call" | custom-call | tf_op jit(solution)/shard_map/sign_step/pallas_call | solution.py:376
  129.6 1.1 write_out.1

commit v7 on v5

--- a/solution.py
+++ b/solution.py
@@ -23,23 +23,23 @@
 LAST = NP - 1
 PART = ((0, 256), (256, 256), (512, 128), (640, 128))
 ORDER = (
-    "LaS3", "RaS1", "LaS0", "prep", "RaS3", "LaS1", "RaS0", "RaS2", "RbS1", "RbS3", "LbS0", "LxS0",
-    "RbS0", "LbS1", "RbS2", "RaS5", "LcS0", "LxS1", "RcS1", "LaS2", "RcS3", "RaS4", "RdS1", "RdS3",
-    "RcS0", "RcS2", "RdS0", "LcS1", "RbS5", "RdS2", "RbS4", "LdS0", "RcS5", "RcS4", "RdS5", "RdS4",
-    "LbS2", "LdS1", "LxS2", "LbS3", "LeS0", "P1_0", "RaQ0", "LcS2", "LxS3", "LeS1", "P1_1", "RaQ1",
-    "RaQ2", "LcS3", "LdS2", "RbQ0", "RbQ1", "LdS3", "P1e_3", "RbQ2", "LeS2", "P1_2", "RaQ3", "RcQ0",
-    "LeS3", "P1_3", "RaQ5", "RaQ4", "RcQ1", "RdQ0", "P2_10", "P2_20", "RdQ1", "RcQ2", "P2_00", "RbQ3",
-    "RdQ2", "P2_01", "RbQ5", "P2_11", "RbQ4", "P2_21", "RcQ3", "RcQ5", "RdQ3", "P2_12", "RcQ4", "P2_02",
-    "RdQ5", "P2_22", "RdQ4", "P2_03", "N0", "RaD0", "LaD0", "P2_13", "N1", "RaD1", "LaD1", "RaD2",
-    "P2_23", "N2", "LaD2", "RaD3", "N3", "RaD5", "RbD0", "RaD4", "LbD0", "LxD0", "RbD1", "RbD2",
-    "LbD1", "LxD1", "RbD3", "RbD5", "LcD0", "LaD3", "RcD0", "RbD4", "RdD0", "P3_10", "RcD1", "P3_20",
-    "LcD1", "LbD2", "LxD2", "RcD2", "P3_00", "RdD1", "RcD3", "RdD2", "P3_11", "RcD4", "RcD5", "P3_21",
-    "RdD3", "P3_22", "RdD5", "RdD4", "P3_23", "W2", "RaW5", "P3_12", "P3_13", "W1", "RaW2", "P3_01",
-    "P3_02", "LdD0", "P3_03", "W0", "RaW0", "RaW1", "RaW3", "RbW5", "LbD3", "RbW2", "LdD1", "LcD2",
-    "LxD3", "RbW0", "RaW4", "RbW1", "LeD0", "RbW3", "LcD3", "RcW5", "RcW2", "RdW5", "RdW2", "RcW0",
-    "LeD1", "RbW4", "RdW0", "P4_00", "RcW1", "LdD2", "P4_10", "RcW3", "RdW1", "P4_01", "RcW4", "RdW3",
-    "P4_02", "LdD3", "P4_11", "P4_12", "RdW4", "P4e_3", "LeD2", "P4_03", "P4_13", "E1", "P4_2", "LeD3",
-    "P4_3", "E3", "E2", "E0",
+    "RaS0", "LaS1", "LaS0", "prep", "RbS0", "RaS4", "RaS3", "RaS5", "LbS1", "LxS1", "RcS0", "RaS1",
+    "RaS2", "LbS0", "LxS0", "RbS4", "LcS1", "RdS0", "RbS3", "RbS5", "RbS1", "LcS0", "LaS2", "RbS2",
+    "RcS4", "RcS3", "RdS4", "RcS5", "RdS3", "RcS1", "RdS5", "RcS2", "RdS1", "LdS1", "RdS2", "LdS0",
+    "LaS3", "LbS2", "LxS2", "LeS1", "P1_1", "RaQ2", "LeS0", "P1_0", "LbS3", "RaQ0", "RaQ1", "RbQ2",
+    "LcS2", "LxS3", "LcS3", "LdS2", "RbQ0", "LdS3", "P1e_3", "RbQ1", "LeS2", "P1_2", "RcQ2", "RaQ3",
+    "LeS3", "P1_3", "RcQ0", "RdQ2", "RaQ5", "RcQ1", "RaQ4", "RdQ0", "P2_20", "RdQ1", "P2_10", "RbQ3",
+    "P2_11", "RbQ5", "P2_00", "RbQ4", "P2_01", "P2_21", "RcQ3", "RcQ5", "RcQ4", "RdQ3", "P2_02", "P2_12",
+    "RdQ5", "RdQ4", "P2_03", "N0", "RaD0", "LaD0", "P2_13", "N1", "RaD2", "P2_22", "P2_23", "N3",
+    "LaD3", "N2", "LaD2", "RaD3", "RbD0", "RaD1", "LbD0", "LxD0", "LaD1", "RaD4", "RaD5", "RbD2",
+    "RbD3", "LbD2", "LxD2", "LcD0", "RcD0", "RdD0", "P3_00", "RbD1", "P3_10", "RbD4", "P3_20", "RbD5",
+    "RcD2", "RcD3", "RdD2", "RcD1", "LbD1", "LxD1", "RdD3", "RcD4", "LcD2", "RcD5", "RdD1", "P3_01",
+    "P3_02", "RdD4", "RdD5", "P3_03", "W0", "RaW0", "P3_21", "P3_22", "P3_11", "LdD0", "LbD3", "P3_12",
+    "P3_13", "LcD1", "LxD3", "W1", "RaW1", "RaW2", "P3_23", "W2", "RaW3", "RaW4", "RbW0", "LdD2",
+    "RbW1", "RaW5", "RbW2", "LeD0", "RbW3", "LcD3", "RbW4", "LdD1", "RcW0", "RcW1", "RdW0", "P4_00",
+    "RdW1", "RbW5", "RcW2", "LeD2", "P4_20", "RcW3", "RdW2", "P4_21", "LdD3", "RcW4", "P4_01", "RcW5",
+    "RdW3", "P4_02", "RdW4", "P4_22", "RdW5", "P4_23", "E2", "P4_03", "E0", "P4e_3", "LeD1", "P4_10",
+    "P4_11", "LeD3", "P4_3", "E3", "P4_12", "P4_13", "E1",
 )
 FIRST = next(int(name[1]) for name in ORDER if name[0] == "E")
 

time: 131 us -> 131 us (level)
  no operation moved by 1% of the time
where the time goes in v7:
time: 131 us
  Pallas kernels  130 us (99%)
    pallas_call x1, Pallas kernels, step(): pl.pallas_call(kernel, out_shape=tuple((pltpu.VMEM(*shape) for shape in s...  129 us

profile of v7, /device:TPU:1, one launch (start us, length us, event | category | flops | bytes accessed | tf_op | source)
XLA Modules:
  0.0 130.7 jit_solution(1727981218411171455)
XLA Ops:
  0.6 128.9 %sign_step.1 = (bf16[768,384]{1,0:T(8,128)(2,1)S(1)}, bf16[768,384]{1,0:T(8,128)(2,1)S(1)}, f32[2,128]{1,0:T(2,128)S(1)}) custom-call(s32[48]{0:T(128)} %band_in.1, s32[48]{0:T(128)} %frag_in.1, bf16[768,384]{1,0:T(8,128)(2,1)} %ham.1, bf16[768,384]{1,0:T(8,128)(2,1)} %deriv.1), custom_call_target="tpu_custom_call" | custom-call | tf_op jit(solution)/shard_map/sign_step/pallas_call | solution.py:373
  129.5 1.0 write_out.1
